TPU v7x, 32 devices: a whole 2x2x4 slice. The times are simulated.
32 devices in a mesh: dp: 8 (over z, y), mp: 4 (over x, core).
Axes of the slice: x: 2, y: 2, z: 4, core: 2. Of those that a mesh axis runs over, the one named last changes fastest.
Arguments:
- tokens: bfloat16 [32768, 512], P(('dp', 'mp')), may hold values from -6 to 6
- cotangent: bfloat16 [32768, 512], P(('dp', 'mp')), may hold values from -6 to 6
- routes: int32 [32768, 8], P(('dp', 'mp')), may hold values from 0 to 23, all different within a row
- starts: int32 [32768], P(('dp', 'mp')), may hold values from 0 to 3072, as said below
- attn_param: float32 [512, 3226], P(('dp', 'mp'))
- attn_first: float32 [512, 3226], P(('dp', 'mp'))
- attn_second: float32 [512, 3226], P(('dp', 'mp')), as said below
- ffn_param: float32 [2, 512, 2048], P(None, 'dp', 'mp')
- ffn_first: float32 [2, 512, 2048], P(None, 'dp', 'mp')
- ffn_second: float32 [2, 512, 2048], P(None, 'dp', 'mp'), as said below
- rates: float32 [7], replicated, as said below
Outputs:
- layer_out: bfloat16 [32768, 512], P(('dp', 'mp'))
- input_grad: float32 [32768, 512], P(('dp', 'mp'))
- attn_grad: float32 [512, 3226], P(('dp', 'mp'))
- attn_second_new: float32 [512, 3226], P(('dp', 'mp'))
- attn_new: float32 [512, 3226], P(('dp', 'mp'))
- ffn_grad: float32 [2, 512, 2048], P(None, 'dp', 'mp')
- ffn_second_new: float32 [2, 512, 2048], P(None, 'dp', 'mp')
- ffn_new: float32 [2, 512, 2048], P(None, 'dp', 'mp')
- grad_norm: float32 [], replicated
- gain_grad: float32 [512, 2], P(('dp', 'mp'))
Inputs may be any that keep to these rules, and one draw needn't show every extreme that they name: `routes`: each row names 8 different experts. `starts`: sequences are contiguous within each group of 4096 tokens; in half of the groups one sequence fills the group, in the others every sequence has 1024 tokens. `attn_second`: positive. `ffn_second`: positive. `rates`: positive.
All inputs are finite; a program needn't handle non-finite values.
Results may differ from a plain program's by a relative error of at most 0.012.
The roundings to bfloat16 on the way count: a program that leaves them out, or rounds other values in their place, can miss the bound.
Values may be sent and summed in bfloat16 or wider, within the bound.
No kernel may reach another device: no remote copies, remote signals or barrier semaphores. Data moves between devices by JAX's collectives and lax.ppermute only.
A program may use at most 128 MiB of HBM per device.

v0:
```python
import jax
import jax.numpy as jnp
from jax import lax
from jax.sharding import PartitionSpec as P

HD = 64
E = 24
TOPK = 8
ADAM_STEP = 7
AC = 3226


NORM_EPS = 1e-05
MASKED = -1e30
CLIP_NORM = 0.1
BETA_FIRST = 0.9
BETA_SECOND = 0.95
ADAM_EPS = 1e-08
WEIGHT_DECAY = 0.1


def cut_along(shard, dim, count):
    before, after = (shard.shape[:dim], shard.shape[dim + 1 :])
    return jnp.moveaxis(shard.reshape(*before, count, -1, *after), dim, 0)


def sum_at_owner(shard, axis, dim):
    count = lax.axis_size(axis)
    blocks = lax.all_to_all(cut_along(shard, dim, count), axis, 0, 0, tiled=True)
    return jnp.sum(blocks.astype(jnp.float32), axis=0)


def contract_last(left, right):
    return lax.dot_general(
        left, right, (((1,), (1,)), ((), ())), preferred_element_type=jnp.float32
    )


def contract_first(left, right):
    return lax.dot_general(
        left, right, (((0,), (0,)), ((), ())), preferred_element_type=jnp.float32
    )


def standardize(values):
    centred = values - jnp.mean(values, -1, keepdims=True)
    factor = lax.rsqrt(jnp.mean(centred * centred, -1, keepdims=True) + NORM_EPS)
    return (centred * factor, factor)


def norm_back(grad_normal, normal, factor):
    return factor * (
        grad_normal
        - jnp.mean(grad_normal, -1, keepdims=True)
        - normal * jnp.mean(grad_normal * normal, -1, keepdims=True)
    )


def silu_slope(pre):
    sigma = jax.nn.sigmoid(pre)
    return sigma * (1.0 + pre * (1.0 - sigma))


def rate_columns(rates):
    span = E * HD
    return jnp.concatenate(
        [
            jnp.full((span,), rates[0]),
            jnp.full((span,), rates[1]),
            jnp.full((2 * HD,), rates[2]),
            jnp.full((E,), rates[3]),
            jnp.full((2,), rates[4]),
        ]
    )


def decay_columns():
    return jnp.concatenate(
        [jnp.full((AC - 2,), WEIGHT_DECAY, jnp.float32), jnp.zeros((2,), jnp.float32)]
    )


def adam_step(param, first, second, grad, rate, decay):
    first_new = BETA_FIRST * first + (1.0 - BETA_FIRST) * grad
    second_new = BETA_SECOND * second + (1.0 - BETA_SECOND) * grad * grad
    first_hat = first_new / (1.0 - BETA_FIRST**ADAM_STEP)
    second_hat = second_new / (1.0 - BETA_SECOND**ADAM_STEP)
    param_new = param - rate * (first_hat / (jnp.sqrt(second_hat) + ADAM_EPS) + decay * param)
    return (second_new, param_new)


def shards(
    tokens,
    cotangent,
    routes,
    starts,
    attn_param,
    attn_first,
    attn_second,
    ffn_param,
    ffn_first,
    ffn_second,
    rates,
):
    local_rows = tokens.shape[0]
    group_rows = local_rows * lax.axis_size("mp")
    model_index = lax.axis_index("mp")
    span = E * HD
    scale = HD ** (-0.5)
    attn_full = lax.all_gather(attn_param.astype(jnp.bfloat16), ("dp", "mp"), axis=0, tiled=True)
    ffn_part = lax.all_gather(ffn_param.astype(jnp.bfloat16), "dp", axis=1, tiled=True)
    w_query = attn_full[:, :span]
    w_output = attn_full[:, span : 2 * span]
    w_keyval = attn_full[:, 2 * span : 2 * span + 2 * HD]
    w_router = attn_full[:, 2 * span + 2 * HD : 2 * span + 2 * HD + E]
    gain_first = attn_full[:, AC - 2].astype(jnp.float32)
    gain_second = attn_full[:, AC - 1].astype(jnp.float32)
    inputs = tokens.astype(jnp.float32)
    normal_first, factor_first = standardize(inputs)
    normed_b = (normal_first * gain_first).astype(jnp.bfloat16)
    query_all = jnp.dot(normed_b, w_query, preferred_element_type=jnp.float32).reshape(
        local_rows, E, HD
    )
    query_b = jnp.take_along_axis(query_all, routes[:, :, None], axis=1).astype(jnp.bfloat16)
    keyval_b = jnp.dot(normed_b, w_keyval, preferred_element_type=jnp.float32).astype(jnp.bfloat16)
    logits = jnp.dot(normed_b, w_router, preferred_element_type=jnp.float32)
    gates = jax.nn.softmax(jnp.take_along_axis(logits, routes, axis=1), axis=-1)
    keyval_all = lax.all_gather(keyval_b, "mp", axis=0, tiled=True)
    key_all = keyval_all[:, :HD]
    value_all = keyval_all[:, HD:]
    stacked = query_b.transpose(1, 0, 2).reshape(TOPK * local_rows, HD)
    lower_of = jnp.tile(starts, TOPK)
    upper_of = model_index * local_rows + jnp.tile(jnp.arange(local_rows, dtype=jnp.int32), TOPK)
    block_rows = min(512, stacked.shape[0])
    blocks = stacked.shape[0] // block_rows
    key_place = jnp.arange(group_rows, dtype=jnp.int32)

    def block_scores(index):
        first = index * block_rows
        query_blk = lax.dynamic_slice_in_dim(stacked, first, block_rows, 0)
        lower = lax.dynamic_slice_in_dim(lower_of, first, block_rows, 0)
        upper = lax.dynamic_slice_in_dim(upper_of, first, block_rows, 0)
        raw = contract_last(query_blk, key_all) * scale
        allowed = (key_place[None, :] >= lower[:, None]) & (key_place[None, :] <= upper[:, None])
        return (query_blk, jnp.where(allowed, raw, MASKED))

    def forward_block(index):
        query_blk, scores = block_scores(index)
        peak = jnp.max(scores, -1)
        expo = jnp.exp(scores - peak[:, None])
        total = jnp.sum(expo, -1)
        probs_b = (expo / total[:, None]).astype(jnp.bfloat16)
        return (
            jnp.dot(probs_b, value_all, preferred_element_type=jnp.float32),
            peak + jnp.log(total),
        )

    attended, log_total = lax.map(forward_block, jnp.arange(blocks))
    attended = attended.reshape(TOPK, local_rows, HD).transpose(1, 0, 2)
    log_total = log_total.reshape(-1)
    onehot = routes[:, :, None] == jnp.arange(E, dtype=jnp.int32)[None, None, :]
    onehot_b = onehot.astype(jnp.bfloat16)
    weighted_b = (gates[:, :, None] * attended).astype(jnp.bfloat16)
    combined_b = (
        jnp.einsum("tke,tkh->teh", onehot_b, weighted_b, preferred_element_type=jnp.float32)
        .astype(jnp.bfloat16)
        .reshape(local_rows, span)
    )
    middle = inputs + contract_last(combined_b, w_output)
    normal_second, factor_second = standardize(middle)
    normed2_b = (normal_second * gain_second).astype(jnp.bfloat16)
    w_up = ffn_part[0]
    w_down = ffn_part[1]
    rows_all = lax.all_gather(normed2_b, "mp", axis=0, tiled=True)
    pre_act = jnp.dot(rows_all, w_up, preferred_element_type=jnp.float32)
    active = jax.nn.silu(pre_act).astype(jnp.bfloat16)
    ffn_branch = lax.psum_scatter(
        contract_last(active, w_down).astype(jnp.bfloat16), "mp", scatter_dimension=0, tiled=True
    ).astype(jnp.float32)
    layer_out = (middle + ffn_branch).astype(jnp.bfloat16)
    out_grad = cotangent.astype(jnp.float32)
    grad_rows = lax.all_gather(cotangent, "mp", axis=0, tiled=True)
    active_grad = jnp.dot(grad_rows, w_down, preferred_element_type=jnp.float32)
    hidden_grad_b = (active_grad * silu_slope(pre_act)).astype(jnp.bfloat16)
    ffn_local = jnp.stack(
        [contract_first(rows_all, hidden_grad_b), contract_first(grad_rows, active)]
    )
    normed2_grad = lax.psum_scatter(
        contract_last(hidden_grad_b, w_up).astype(jnp.bfloat16),
        "mp",
        scatter_dimension=0,
        tiled=True,
    ).astype(jnp.float32)
    middle_grad = out_grad + norm_back(normed2_grad * gain_second, normal_second, factor_second)
    gain2_grad = jnp.sum(normed2_grad * normal_second, 0)
    middle_b = middle_grad.astype(jnp.bfloat16)
    combined_grad = jnp.dot(middle_b, w_output, preferred_element_type=jnp.float32).reshape(
        local_rows, E, HD
    )
    grad_output_proj = contract_first(middle_b, combined_b)
    picked = jnp.take_along_axis(combined_grad, routes[:, :, None], axis=1)
    gate_grad = jnp.sum(attended * picked, -1)
    attended_grad_b = (gates[:, :, None] * picked).astype(jnp.bfloat16)
    chosen_grad = gates * (gate_grad - jnp.sum(gates * gate_grad, -1, keepdims=True))
    logit_grad_b = jnp.sum(onehot.astype(jnp.float32) * chosen_grad[:, :, None], 1).astype(
        jnp.bfloat16
    )
    stacked_grad = attended_grad_b.transpose(1, 0, 2).reshape(TOPK * local_rows, HD)

    def backward_block(carry, index):
        key_acc, value_acc = carry
        query_blk, scores = block_scores(index)
        log_blk = lax.dynamic_slice_in_dim(log_total, index * block_rows, block_rows, 0)
        grad_blk = lax.dynamic_slice_in_dim(stacked_grad, index * block_rows, block_rows, 0)
        probs = jnp.exp(scores - log_blk[:, None])
        value_acc = value_acc + contract_first(probs.astype(jnp.bfloat16), grad_blk)
        prob_grad = contract_last(grad_blk, value_all)
        inner = jnp.sum(probs * prob_grad, -1, keepdims=True)
        score_grad_b = (probs * (prob_grad - inner) * scale).astype(jnp.bfloat16)
        key_acc = key_acc + contract_first(score_grad_b, query_blk)
        return (
            (key_acc, value_acc),
            jnp.dot(score_grad_b, key_all, preferred_element_type=jnp.float32),
        )

    zero_rows = jnp.zeros((group_rows, HD), jnp.float32)
    (key_acc, value_acc), query_grads = lax.scan(
        backward_block, (zero_rows, zero_rows), jnp.arange(blocks)
    )
    query_grad_b = query_grads.reshape(TOPK, local_rows, HD).transpose(1, 0, 2).astype(jnp.bfloat16)
    query_all_grad_b = (
        jnp.einsum("tke,tkh->teh", onehot_b, query_grad_b, preferred_element_type=jnp.float32)
        .astype(jnp.bfloat16)
        .reshape(local_rows, span)
    )
    keyval_grad = lax.psum_scatter(
        jnp.concatenate([key_acc, value_acc], 1).astype(jnp.bfloat16),
        "mp",
        scatter_dimension=0,
        tiled=True,
    )
    normed_grad = (
        contract_last(query_all_grad_b, w_query)
        + contract_last(keyval_grad, w_keyval)
        + contract_last(logit_grad_b, w_router)
    )
    gain1_grad = jnp.sum(normed_grad * normal_first, 0)
    input_grad = middle_grad + norm_back(normed_grad * gain_first, normal_first, factor_first)
    attn_local = jnp.concatenate(
        [
            contract_first(normed_b, query_all_grad_b),
            grad_output_proj,
            contract_first(normed_b, keyval_grad),
            contract_first(normed_b, logit_grad_b),
            gain1_grad[:, None],
            gain2_grad[:, None],
        ],
        1,
    )
    attn_raw = lax.psum_scatter(attn_local, ("dp", "mp"), scatter_dimension=0, tiled=True)
    ffn_raw = sum_at_owner(ffn_local.astype(jnp.bfloat16), "dp", 1)
    squares = jnp.sum(attn_raw * attn_raw) + jnp.sum(ffn_raw * ffn_raw)
    grad_norm = jnp.sqrt(lax.psum(squares, ("dp", "mp")))
    factor = jnp.minimum(1.0, CLIP_NORM / grad_norm)
    attn_grad = attn_raw * factor
    ffn_grad = ffn_raw * factor
    attn_second_new, attn_new = adam_step(
        attn_param,
        attn_first,
        attn_second,
        attn_grad,
        rate_columns(rates)[None, :],
        decay_columns()[None, :],
    )
    ffn_rates = jnp.stack([rates[5], rates[6]])[:, None, None]
    ffn_second_new, ffn_new = adam_step(
        ffn_param, ffn_first, ffn_second, ffn_grad, ffn_rates, WEIGHT_DECAY
    )
    gain_grad = attn_grad[:, AC - 2 :]
    return (
        layer_out,
        input_grad,
        attn_grad,
        attn_second_new,
        attn_new,
        ffn_grad,
        ffn_second_new,
        ffn_new,
        grad_norm,
        gain_grad,
    )


def solution(mesh):
    placed = (
        P(("dp", "mp"), None),
        P(("dp", "mp"), None),
        P(("dp", "mp"), None),
        P(("dp", "mp")),
        P(("dp", "mp"), None),
        P(("dp", "mp"), None),
        P(("dp", "mp"), None),
        P(None, "dp", "mp"),
        P(None, "dp", "mp"),
        P(None, "dp", "mp"),
        P(),
    )
    return jax.shard_map(
        shards,
        mesh=mesh,
        in_specs=placed,
        out_specs=(
            P(("dp", "mp"), None),
            P(("dp", "mp"), None),
            P(("dp", "mp"), None),
            P(("dp", "mp"), None),
            P(("dp", "mp"), None),
            P(None, "dp", "mp"),
            P(None, "dp", "mp"),
            P(None, "dp", "mp"),
            P(),
            P(("dp", "mp"), None),
        ),
        check_vma=False,
    )
```

profile of v0, /device:TPU:1, one launch (start us, length us, event | category | flops | bytes accessed | tf_op | source)
XLA Modules:
  0.0 1693.7 jit_solution(9233913597722293800)
XLA Ops:
  11.0 62.7 %all-gather.6.cloned.1.call-done = bf16[512,3226]{1,0:T(8,128)(2,1)} async-done(((bf16[16,3226]{1,0:T(8,128)(2,1)}), bf16[512,3226]{1,0:T(8,128)(2,1)}) %all-gather.6.cloned.1.call-update) | async-done | bytes 3303440 | tf_op jit(solution)/shard_map/all_gather | solution.py:110
  84.9 65.7 %gather_fusion = f32[8192]{0:T(1024)S(1)} fusion(f32[1024,24]{0,1:T(8,128)S(1)} %fusion.74, s32[8192]{0:T(1024)S(1)} %reshape.218), kind=kCustom, calls=%fused_computation.2 | custom fusion | bytes 131072 | tf_op jit(solution)/shard_map/jit(take_along_axis)/gather | solution.py:127
  161.1 98.4 %gather_fusion.1 = bf16[8192,64]{1,0:T(8,128)(2,1)S(1)} fusion(bf16[1024,24,64]{2,1,0:T(8,128)(2,1)} %copy.78, s32[8192]{0:T(1024)S(1)} %copy-done.2), kind=kCustom, calls=%fused_computation.clone | custom fusion | bytes 2162688 | tf_op jit(solution)/shard_map/jit(take_along_axis)/gather | solution.py:124
  266.4 291.6 %while.30 = (s32[]{:T(128)}, f32[16,512,64]{1,0,2:T(8,128)}, f32[16,512]{1,0:T(8,128)S(1)}, s32[16]{0:T(128)S(1)}, s32[8192]{0:T(1024)}, /*index=5*/s32[8192]{0:...) while((s32[]{:T(128)}, f32[16,512,64]{1,0,2:T(8,128)}, ...), condition=%wide.region_7.9_spmd.clone.clone, body=%wide.region_4.8_spmd.clone.clone.sunk | while | flops 559939072 | bytes 60588264 | solution.py:158
  592.5 32.6 %all-gather.10.cloned.1.call-done = bf16[4096,512]{0,1:T(8,128)(2,1)} async-done(((bf16[1024,512]{0,1:T(8,128)(2,1)}), bf16[4096,512]{0,1:T(8,128)(2,1)}) %all-gather.10.cloned.1.call-update) | async-done | bytes 4194320 | tf_op jit(solution)/shard_map/all_gather | solution.py:174
  625.1 11.2 multiply_convert_fusion.2
  636.3 24.7 %all-gather.14.cloned.1.call-done = bf16[4096,512]{1,0:T(8,128)(2,1)} async-done(((bf16[1024,512]{1,0:T(8,128)(2,1)}), bf16[4096,512]{1,0:T(8,128)(2,1)}) %all-gather.14.cloned.1.call-update) | async-done | bytes 4194320 | tf_op jit(solution)/shard_map/all_gather | solution.py:182
  684.5 34.5 %reduce-scatter.7.cloned.1.call-done = bf16[1024,512]{0,1:T(8,128)(2,1)} async-done(((bf16[4096,512]{0,1:T(8,128)(2,1)}), bf16[1024,512]{0,1:T(8,128)(2,1)}) %reduce-scatter.7.cloned.1.call-update) | async-done | bytes 1048592 | tf_op jit(solution)/shard_map/reduce_scatter | solution.py:188
  722.3 43.9 %reduce-scatter.5.cloned.1.call-done = bf16[1024,512]{0,1:T(8,128)(2,1)} async-done(((bf16[4096,512]{0,1:T(8,128)(2,1)}), bf16[1024,512]{0,1:T(8,128)(2,1)}) %reduce-scatter.5.cloned.1.call-update) | async-done | bytes 1048592 | tf_op jit(solution)/shard_map/reduce_scatter | solution.py:177
  787.2 119.1 %gather_fusion.2 = f32[8192,64]{1,0:T(8,128)} fusion(f32[1024,24,64]{2,1,0:T(8,128)} %copy.88, s32[8192]{0:T(1024)S(1)} %copy-done.3), kind=kCustom, calls=%fused_computation.1.clone | custom fusion | bytes 4259840 | tf_op jit(solution)/shard_map/jit(take_along_axis)/gather | solution.py:201
  917.6 515.3 %while.31 = (s32[]{:T(128)}, f32[4096,64]{0,1:T(8,128)S(1)}, f32[4096,64]{0,1:T(8,128)S(1)}, bf16[16,512,64]{1,2,0:T(8,128)(2,1)}, s32[16]{0:T(128)S(1)}, /*inde...) while((s32[]{:T(128)}, f32[4096,64]{0,1:T(8,128)S(1)}, ...), condition=%wide.region_16.18_spmd.clone.clone, body=%wide.region_14.17_spmd.clone.clone.sunk | while | flops 1370488320 | bytes 139090768 | solution.py:227
  929.8 10.0 multiply_convert_fusion.6
  962.0 10.0 multiply_convert_fusion.6
  994.1 10.0 multiply_convert_fusion.6
  1026.3 10.0 multiply_convert_fusion.6
  1058.5 10.0 multiply_convert_fusion.6
  1090.7 10.0 multiply_convert_fusion.6
  1122.9 10.0 multiply_convert_fusion.6
  1219.5 10.0 multiply_convert_fusion.6
  1251.7 10.0 multiply_convert_fusion.6
  1380.5 10.0 multiply_convert_fusion.6
  1509.1 24.5 %all-to-all-done = bf16[8,2,64,512]{3,2,1,0:T(8,128)(2,1)} async-done(((bf16[8,2,64,512]{3,2,1,0:T(8,128)(2,1)}), bf16[8,2,64,512]{3,2,1,0:T(8,128)(2,1)}, u32[]{:S(2)}, u32[]{:S(2)}) %all-to-all-start) | async-done | bytes 1048608 | tf_op jit(solution)/shard_map/all_to_all | solution.py:29
  1541.7 93.1 %reduce-scatter.11.cloned.1.call-done = f32[16,3226]{1,0:T(8,128)} async-done(((f32[512,3226]{1,0:T(8,128)}), f32[16,3226]{1,0:T(8,128)}) %reduce-scatter.11.cloned.1.call-update) | async-done | bytes 206480 | tf_op jit(solution)/shard_map/reduce_scatter | solution.py:260
  1640.7 41.7 %psum.7 = f32[]{:T(128)} all-reduce(f32[]{:T(128)S(6)} %add.160), channel_id=1, replica_groups=mesh['dp'=8,'mp'=4] {'dp','mp'}, use_global_device_ids=true, to_apply=%region_29.31 | all-reduce | flops 1 | bytes 8 | tf_op jit(solution)/shard_map/psum | solution.py:263
  (668 shorter events, 900.4 us)
Async XLA Ops:
  7.2 75.9 %copy-start = (s32[1024]{0:T(1024)S(1)}, s32[1024]{0:T(1024)}, u32[]{:S(2)}) copy-start(s32[1024]{0:T(1024)} %param.20) | copy-start | bytes 12292
  7.2 66.5 %all-gather.6.cloned.1.call-start = ((), (), s32[]{:S(2)}) async-start(), calls=%async_computation.5 | async-start | bytes 3514368 | tf_op jit(solution)/shard_map/all_gather | solution.py:110
  8.9 255.6 %all-gather.8.cloned.1.call-start = ((), (), s32[]{:S(2)}) async-start(), calls=%async_computation.6 | async-start | bytes 1310720 | tf_op jit(solution)/shard_map/all_gather | solution.py:128
  10.4 69.2 %copy-start.7 = (bf16[1024,512]{0,1:T(8,128)(2,1)}, bf16[1024,512]{0,1:T(8,128)(2,1)S(1)}, u32[]{:S(2)}) copy-start(bf16[1024,512]{0,1:T(8,128)(2,1)S(1)} %copy.71) | copy-start | bytes 3145732
  10.6 70.2 %copy-start.37 = (f32[1024]{0:T(1024)}, f32[1024]{0:T(1024)S(1)}, u32[]{:S(2)}) copy-start(f32[1024]{0:T(1024)S(1)} %broadcast_multiply_fusion.7) | copy-start | bytes 12292
  11.0 70.3 %copy-start.41 = (f32[1024]{0:T(1024)}, f32[1024]{0:T(1024)S(1)}, u32[]{:S(2)}) copy-start(f32[1024]{0:T(1024)S(1)} %add_rsqrt_fusion.1) | copy-start | bytes 12292
  76.4 74.2 %copy-start.13 = (bf16[1024,512]{0,1:T(8,128)(2,1)}, bf16[1024,512]{0,1:T(8,128)(2,1)S(1)}, u32[]{:S(2)}) copy-start(bf16[1024,512]{0,1:T(8,128)(2,1)S(1)} %fusion.36) | copy-start | bytes 3145732
  78.7 513.7 %all-gather.12.cloned.1.call-start = ((), (), s32[]{:S(2)}) async-start(), calls=%async_computation.8 | async-start | bytes 1179648 | tf_op jit(solution)/shard_map/all_gather | solution.py:111
  79.5 545.6 %all-gather.10.cloned.1.call-start = ((), (), s32[]{:S(2)}) async-start(), calls=%async_computation.7 | async-start | bytes 5242880 | tf_op jit(solution)/shard_map/all_gather | solution.py:174
  79.6 71.0 %copy-start.39 = (pred[1024,8]{0,1:T(8,128)(4,1)}, pred[1024,8]{0,1:T(8,128)(4,1)S(1)}, u32[]{:S(2)}) copy-start(pred[1024,8]{0,1:T(8,128)(4,1)S(1)} %and_bitcast_fusion) | copy-start | bytes 24580
  161.1 98.4 %copy-start.31 = (pred[1024,8]{1,0:T(8,128)(4,1)S(1)}, pred[1024,8]{1,0:T(8,128)(4,1)}, u32[]{:S(2)}) copy-start(pred[1024,8]{1,0:T(8,128)(4,1)} %copy.75) | copy-start | bytes 24580
  591.8 69.2 %all-gather.14.cloned.1.call-start = ((), (), s32[]{:S(2)}) async-start(), calls=%async_computation.10 | async-start | bytes 5242880 | tf_op jit(solution)/shard_map/all_gather | solution.py:182
  592.4 126.5 %reduce-scatter.7.cloned.1.call-start = ((), (), s32[]{:S(2)}) async-start(), calls=%async_computation.11 | async-start | bytes 5242880 | tf_op jit(solution)/shard_map/reduce_scatter | solution.py:188
  674.7 91.5 %reduce-scatter.5.cloned.1.call-start = ((), (), s32[]{:S(2)}) async-start(), calls=%async_computation.9 | async-start | bytes 5242880 | tf_op jit(solution)/shard_map/reduce_scatter | solution.py:177
  681.4 795.3 %reduce-scatter.9.cloned.1.call-start = ((), (), s32[]{:S(2)}) async-start(), calls=%async_computation.12 | async-start | bytes 1310720 | tf_op jit(solution)/shard_map/reduce_scatter | solution.py:236
  1434.1 200.7 %reduce-scatter.11.cloned.1.call-start = ((), (), s32[]{:S(2)}) async-start(), calls=%async_computation.13 | async-start | bytes 7028736 | tf_op jit(solution)/shard_map/reduce_scatter | solution.py:260
  1499.6 34.0 %all-to-all-start = ((bf16[8,2,64,512]{3,2,1,0:T(8,128)(2,1)}), bf16[8,2,64,512]{3,2,1,0:T(8,128)(2,1)}, u32[]{:S(2)}, u32[]{:S(2)}) async-start(bf16[8,2,64,512]{3,2,1,0:T(8,128)(2,1)} %maximum_bitcast_fusion), calls=%async_computation.4 | async-start | bytes 2097152 | tf_op jit(solution)/shard_map/all_to_all | solution.py:29
  1541.6 141.4 %copy-start.29 = (f32[16,3226]{1,0:T(8,128)S(1)}, f32[16,3226]{1,0:T(8,128)}, u32[]{:S(2)}) copy-start(f32[16,3226]{1,0:T(8,128)} %param.21) | copy-start | bytes 619396
  1541.6 141.4 %copy-start.35 = (f32[16,3226]{1,0:T(8,128)S(1)}, f32[16,3226]{1,0:T(8,128)}, u32[]{:S(2)}) copy-start(f32[16,3226]{1,0:T(8,128)} %param.22) | copy-start | bytes 619396
  1541.6 141.5 %copy-start.36 = (f32[16,3226]{1,0:T(8,128)S(1)}, f32[16,3226]{1,0:T(8,128)}, u32[]{:S(2)}) copy-start(f32[16,3226]{1,0:T(8,128)} %param.23) | copy-start | bytes 619396
  1541.6 141.5 %copy-start.47 = (f32[3226]{0:T(1024)S(1)}, f32[3226]{0:T(1024)}, u32[]{:S(2)}) copy-start(f32[3226]{0:T(1024)} %constant.127.clone.1) | copy-start | bytes 38716
  1541.7 143.1 %copy-start.26 = (f32[2,64,512]{2,1,0:T(8,128)S(1)}, f32[2,64,512]{2,1,0:T(8,128)}, u32[]{:S(2)}) copy-start(f32[2,64,512]{2,1,0:T(8,128)} %param.24) | copy-start | bytes 786436
  1541.7 143.1 %copy-start.32 = (f32[2,64,512]{2,1,0:T(8,128)S(1)}, f32[2,64,512]{2,1,0:T(8,128)}, u32[]{:S(2)}) copy-start(f32[2,64,512]{2,1,0:T(8,128)} %param.25) | copy-start | bytes 786436
  1541.7 143.1 %copy-start.33 = (f32[2,64,512]{2,1,0:T(8,128)S(1)}, f32[2,64,512]{2,1,0:T(8,128)}, u32[]{:S(2)}) copy-start(f32[2,64,512]{2,1,0:T(8,128)} %param.26) | copy-start | bytes 786436
  (100 other events, 926.8 us)
Sparse Core Ops, SparseCore 0:
  11.4 62.2 all-gather.5
  78.9 15.4 all-gather.7
  97.1 38.7 all-gather.11
  591.9 33.0 all-gather.9
  626.5 34.4 all-gather.13
  674.8 44.0 reduce-scatter.6
  721.6 44.5 reduce-scatter.4
  1434.3 25.0 reduce-scatter.8
  1490.3 144.4 reduce-scatter.10
where the time goes:
time: 1710 us; the launch traced here: 1690 us
  local copies, waits for them, and re-layouts  534 us (31%)
  matrix products  531 us (31%)
  waiting for transfers between devices  317 us (19%)
  other arithmetic  223 us (13%)
  blocking collectives  41.7 us (2%)
  loops' own time  22.8 us (1%)
  between operations  18.1 us (1%)
    dot_general x54, matrix products, contract_last(): lax.dot_general(left, right, (((1,), (1,)), ((), ())), preferred_element_...  231 us
    convert_element_type x16, other arithmetic, backward_block(): score_grad_b = (probs * (prob_grad - inner) * scale).astype(jnp.bfloat16)  161 us
    gather x2, local copies, waits for them, and re-layouts, shards(): picked = jnp.take_along_axis(combined_grad, routes[:, :, None], axis=1)  124 us
    dot_general x38, matrix products, contract_first(): lax.dot_general(left, right, (((0,), (0,)), ((), ())), preferred_element_...  101 us
    gather x3, local copies, waits for them, and re-layouts, shards(): jnp.take_along_axis(query_all, routes[:, :, None], axis=1)  99.4 us
    reduce_scatter x1, waiting for transfers between devices, shards(): lax.psum_scatter(attn_local, ('dp', 'mp'), scatter_dimension=0, tiled=True)  93.1 us
    dot_general x16, matrix products, backward_block(): jnp.dot(score_grad_b, key_all, preferred_element_type=jnp.float32)  77.5 us
    dot_general x16, matrix products, forward_block(): jnp.dot(probs_b, value_all, preferred_element_type=jnp.float32)  72.4 us
  transfers between devices with their start and end apart: 10, of which 7 were waited for; matrix products, arithmetic and copies ran while one was open for 33% of the time, Pallas kernels for 0%

commit v1 on v0

v1 whole, which is shorter than its diff:
```python
import functools
import math

import jax
import jax.numpy as jnp
from jax import lax
from jax.experimental import pallas as pl
from jax.experimental.pallas import tpu as pltpu
from jax.sharding import PartitionSpec as P

HD = 64
E = 24
TOPK = 8
ADAM_STEP = 7
AC = 3226
SPAN = E * HD
PAIRS = E // 2
LANES = 128

NORM_EPS = 1e-05
MASKED = -1e30
CLIP_NORM = 0.1
BETA_FIRST = 0.9
BETA_SECOND = 0.95
ADAM_EPS = 1e-08
WEIGHT_DECAY = 0.1

SCALE = HD ** (-0.5)
LOG2E = math.log2(math.e)
SAFE_SCORE = 40.0
SAFE_VALUE = 1e15
VMEM = 58 << 20

F32 = jnp.float32
BF16 = jnp.bfloat16


def dot(left, right):
    return jnp.dot(left, right, preferred_element_type=F32)


def dot_last(left, right):
    return lax.dot_general(left, right, (((1,), (1,)), ((), ())), preferred_element_type=F32)


def turned(values):
    return values.astype(F32).T.astype(values.dtype)


def standardize(values):
    centred = values - jnp.mean(values, -1, keepdims=True)
    factor = lax.rsqrt(jnp.mean(centred * centred, -1, keepdims=True) + NORM_EPS)
    return (centred * factor, factor)


def norm_back(grad_normal, normal, factor):
    return factor * (
        grad_normal
        - jnp.mean(grad_normal, -1, keepdims=True)
        - normal * jnp.mean(grad_normal * normal, -1, keepdims=True)
    )


def lane_index(rows):
    return lax.broadcasted_iota(jnp.int32, (rows, LANES), 1)


def column(values, index, rows):
    return jnp.broadcast_to(values[:, index : index + 1], (rows, LANES))


def pick_pairs(table, chosen):
    picked = jnp.zeros(chosen.shape, F32)
    for pair in range(PAIRS):
        picked = jnp.where(chosen == 2 * pair, table[:, pair * LANES : (pair + 1) * LANES], picked)
    return picked


def gains_of(tail):
    return tail.astype(F32).T


def pre_kernel(x_ref, routes_ref, w_ref, h_ref, q_ref, kv_ref, gate_ref):
    rows = x_ref.shape[0]
    gain = gains_of(w_ref[:, SPAN + LANES :])[E : E + 1]
    normal, _ = standardize(x_ref[...].astype(F32))
    h = (normal * gain).astype(BF16)
    h_ref[...] = h
    proj = dot(h, w_ref[...])
    kv_ref[...] = proj[:, SPAN : SPAN + LANES].astype(BF16)
    logits = proj[:, SPAN + LANES :]
    routes = routes_ref[...]
    lane = lane_index(rows)
    half = (lane >= HD).astype(jnp.int32)
    chosen = jnp.zeros((rows, LANES), jnp.bool_)
    for slot in range(TOPK):
        route = column(routes, slot, rows)
        q_ref[slot] = pick_pairs(proj, route - half).astype(BF16)
        chosen = chosen | (lane == route)
    peak = jnp.max(jnp.where(chosen, logits, MASKED), -1, keepdims=True)
    expo = jnp.where(chosen, jnp.exp(jnp.where(chosen, logits - peak, 0.0)), 0.0)
    dense = expo / jnp.sum(expo, -1, keepdims=True)
    gates = jnp.zeros((rows, LANES), F32)
    for slot in range(TOPK):
        hit = jnp.where(lane == column(routes, slot, rows), dense, 0.0)
        gates = jnp.where(lane == slot, jnp.sum(hit, -1, keepdims=True), gates)
    gate_ref[...] = gates


def pre_call(x, routes, weights, tile=256):
    rows, width = x.shape
    cols = weights.shape[1]
    return pl.pallas_call(
        pre_kernel,
        grid=(rows // tile,),
        in_specs=[
            pl.BlockSpec((tile, width), lambda i: (i, 0)),
            pl.BlockSpec((tile, TOPK), lambda i: (i, 0)),
            pl.BlockSpec((width, cols), lambda i: (0, 0)),
        ],
        out_specs=[
            pl.BlockSpec((tile, width), lambda i: (i, 0)),
            pl.BlockSpec((TOPK, tile, LANES), lambda i: (0, i, 0)),
            pl.BlockSpec((tile, LANES), lambda i: (i, 0)),
            pl.BlockSpec((tile, LANES), lambda i: (i, 0)),
        ],
        out_shape=[
            jax.ShapeDtypeStruct((rows, width), BF16),
            jax.ShapeDtypeStruct((TOPK, rows, LANES), BF16),
            jax.ShapeDtypeStruct((rows, LANES), BF16),
            jax.ShapeDtypeStruct((rows, LANES), F32),
        ],
        compiler_params=pltpu.CompilerParams(vmem_limit_bytes=VMEM),
        cost_estimate=pl.CostEstimate(
            flops=2 * rows * width * cols, bytes_accessed=8 * rows * width + 2 * width * cols, transcendentals=0
        ),
        name="project",
    )(x, routes, weights)


def spread_keyval(kv_ref, key_ref, value_ref, with_ones):
    block = kv_ref.shape[1]
    devices = kv_ref.shape[0] // 2
    low_half = lane_index(block) < HD
    for index in range(2 * devices):
        place = index // 2 if index % 2 == 0 else 2 * devices - 1 - index // 2
        rows = kv_ref[index].astype(F32)
        rolled = pltpu.roll(rows, HD, 1)
        span = pl.ds(place * block, block)
        key_ref[span, :] = jnp.where(low_half, rows, rolled).astype(BF16)
        value_ref[span, :LANES] = jnp.where(low_half, rolled, rows).astype(BF16)
        if with_ones:
            value_ref[span, LANES:] = jnp.ones((block, LANES), BF16)


def attend_kernel(place_ref, q_ref, kv_ref, o_ref, log_ref, key_ref, value_ref, acc_ref, peak_ref, bound_ref):
    step = pl.program_id(0)
    slots, tile, _ = q_ref.shape
    rows = slots * tile
    width = 512

    @pl.when(step == 0)
    def _():
        spread_keyval(kv_ref, key_ref, value_ref, True)
        keys = key_ref[...].astype(F32)
        bound_ref[0] = jnp.max(jnp.sum(keys * keys, -1, keepdims=True)) * 0.5
        bound_ref[1] = jnp.max(jnp.abs(value_ref[:, :LANES].astype(F32)))

    here = place_ref[0, step]
    lower = place_ref[1, step]
    q = q_ref[...].reshape(rows, LANES)
    qf = q.astype(F32)
    longest = jnp.max(jnp.sum(qf * qf, -1, keepdims=True))
    plain = (longest * bound_ref[0] <= (SAFE_SCORE / SCALE) ** 2) & (bound_ref[1] <= SAFE_VALUE)
    full = (here - lower) // width
    last = pl.multiple_of(lower + full * width, width)
    token = lax.broadcasted_iota(jnp.int32, (tile, width), 0) + here
    allowed = (lax.broadcasted_iota(jnp.int32, (tile, width), 1) + last) <= token
    allowed = jnp.broadcast_to(allowed[None], (slots, tile, width)).reshape(rows, width)

    @pl.when(plain)
    def _():
        expo = jnp.exp2(dot_last(q, key_ref[pl.ds(last, width), :]) * (SCALE * LOG2E))
        expo = jnp.where(allowed, expo, 0.0).astype(BF16)
        acc_ref[...] = dot(expo, value_ref[pl.ds(last, width), :])

        def body(index, carry):
            span = pl.ds(pl.multiple_of(lower + index * width, width), width)
            expo = jnp.exp2(dot_last(q, key_ref[span, :]) * (SCALE * LOG2E)).astype(BF16)
            acc_ref[...] += dot(expo, value_ref[span, :])
            return carry

        lax.fori_loop(0, full, body, 0)
        peak_ref[...] = jnp.zeros_like(peak_ref)

    @pl.when(jnp.logical_not(plain))
    def _():
        def scaled(span):
            return dot_last(q, key_ref[span, :]) * (SCALE * LOG2E)

        scores = jnp.where(allowed, scaled(pl.ds(last, width)), MASKED)
        peak = jnp.max(scores, -1, keepdims=True)
        peak_ref[...] = jnp.broadcast_to(peak, (rows, LANES))
        acc_ref[...] = dot(jnp.exp2(scores - peak).astype(BF16), value_ref[pl.ds(last, width), :])

        def body(index, carry):
            span = pl.ds(pl.multiple_of(lower + index * width, width), width)
            scores = scaled(span)
            before = peak_ref[:, :1]
            peak = jnp.maximum(before, jnp.max(scores, -1, keepdims=True))
            peak_ref[...] = jnp.broadcast_to(peak, (rows, LANES))
            expo = jnp.exp2(scores - peak).astype(BF16)
            acc_ref[...] = acc_ref[...] * jnp.exp2(before - peak) + dot(expo, value_ref[span, :])
            return carry

        lax.fori_loop(0, full, body, 0)

    total = acc_ref[:, LANES:]
    o_ref[...] = (acc_ref[:, :LANES] / total).reshape(slots, tile, LANES)
    logs = (peak_ref[...] + jnp.log2(total)).reshape(slots, tile, LANES)
    lane = lane_index(tile)
    packed = jnp.zeros((tile, LANES), F32)
    for slot in range(slots):
        packed = jnp.where(lane == slot, logs[slot], packed)
    log_ref[...] = packed


def attend_call(place, q, kv, tile=128):
    slots, rows, _ = q.shape
    count = kv.shape[0] * kv.shape[1]
    return pl.pallas_call(
        attend_kernel,
        grid_spec=pltpu.PrefetchScalarGridSpec(
            num_scalar_prefetch=1,
            grid=(rows // tile,),
            in_specs=[
                pl.BlockSpec((slots, tile, LANES), lambda i, s: (0, i, 0)),
                pl.BlockSpec(kv.shape, lambda i, s: (0, 0, 0)),
            ],
            out_specs=[
                pl.BlockSpec((slots, tile, LANES), lambda i, s: (0, i, 0)),
                pl.BlockSpec((tile, LANES), lambda i, s: (i, 0)),
            ],
            scratch_shapes=[
                pltpu.VMEM((count, LANES), BF16),
                pltpu.VMEM((count, 2 * LANES), BF16),
                pltpu.VMEM((slots * tile, 2 * LANES), F32),
                pltpu.VMEM((slots * tile, LANES), F32),
                pltpu.SMEM((2,), F32),
            ],
        ),
        out_shape=[
            jax.ShapeDtypeStruct((slots, rows, LANES), F32),
            jax.ShapeDtypeStruct((rows, LANES), F32),
        ],
        compiler_params=pltpu.CompilerParams(vmem_limit_bytes=VMEM),
        cost_estimate=pl.CostEstimate(
            flops=8 * slots * rows * count * LANES, bytes_accessed=8 * slots * rows * LANES, transcendentals=0
        ),
        name="attend",
    )(place, q, kv)


def attend_back_kernel(
    place_ref, q_ref, do_ref, log_ref, delta_ref, routes_ref, h_ref, dlog_ref, kv_ref, w_ref,
    dh_ref, gq_ref, dkv_ref,
    key_ref, value_ref, dq_ref, dkey_ref, dvalue_ref, all_ref, turn_ref,
):
    step = pl.program_id(0)
    slots, tile, _ = q_ref.shape
    rows = slots * tile
    width = 512

    @pl.when(step == 0)
    def _():
        spread_keyval(kv_ref, key_ref, value_ref, False)
        dkey_ref[...] = jnp.zeros_like(dkey_ref)
        dvalue_ref[...] = jnp.zeros_like(dvalue_ref)

    here = place_ref[0, step]
    lower = place_ref[1, step]
    q = q_ref[...].reshape(rows, LANES)
    do = do_ref[...].reshape(rows, LANES)
    q_turned = turned(q)
    do_turned = turned(do)
    logs = log_ref[...]
    deltas = delta_ref[...]
    logs = jnp.concatenate([column(logs, slot, tile) for slot in range(slots)], 0)
    deltas = jnp.concatenate([column(deltas, slot, tile) for slot in range(slots)], 0)
    full = (here - lower) // width
    last = pl.multiple_of(lower + full * width, width)
    token = lax.broadcasted_iota(jnp.int32, (tile, width), 0) + here
    allowed = (lax.broadcasted_iota(jnp.int32, (tile, width), 1) + last) <= token
    allowed = jnp.broadcast_to(allowed[None], (slots, tile, width)).reshape(rows, width)

    def wide(values):
        return jnp.concatenate([values] * (width // LANES), 1)

    def one(first, masked):
        span = pl.ds(first, width)
        keys = key_ref[span, :]
        scores = dot_last(q, keys)
        probs = jnp.exp2(scores * (SCALE * LOG2E) - wide(logs))
        if masked:
            probs = jnp.where(allowed, probs, 0.0)
        dprobs = dot_last(do, value_ref[span, :])
        dscores = (probs * (dprobs - wide(deltas))).astype(BF16)
        dvalue_ref[:, span] += dot(do_turned, probs.astype(BF16))
        dkey_ref[:, span] += dot(q_turned, dscores)
        return dot(dscores, keys)

    dq_ref[...] = one(last, True)

    def body(index, carry):
        dq_ref[...] += one(pl.multiple_of(lower + index * width, width), False)
        return carry

    lax.fori_loop(0, full, body, 0)

    routes = routes_ref[...]
    half = (lane_index(tile) >= HD).astype(jnp.int32)
    chosen = [column(routes, slot, tile) - half for slot in range(slots)]
    dq = (dq_ref[...] * SCALE).reshape(slots, tile, LANES)
    mine = pl.ds(pl.multiple_of(step * tile, tile), tile)
    for pair in range(PAIRS):
        total = jnp.zeros((tile, LANES), F32)
        for slot in range(slots):
            total = jnp.where(chosen[slot] == 2 * pair, dq[slot], total)
        all_ref[mine, pair * LANES : (pair + 1) * LANES] = total.astype(BF16)
    turn_ref[:, mine] = turned(h_ref[...])
    dh_ref[...] = dot_last(all_ref[mine, :], w_ref[:, :SPAN]) + dot_last(dlog_ref[...], w_ref[:, SPAN + LANES :])

    @pl.when(step == pl.num_programs(0) - 1)
    def _():
        gq_ref[...] = dot(turn_ref[...], all_ref[...]).astype(BF16)
        block = dkv_ref.shape[1]
        devices = dkv_ref.shape[0] // 2
        for index in range(2 * devices):
            place = index // 2 if index % 2 == 0 else 2 * devices - 1 - index // 2
            span = slice(place * block, (place + 1) * block)
            dkeys = (dkey_ref[:HD, span] + dkey_ref[HD:, span]) * SCALE
            dvalues = dvalue_ref[:HD, span] + dvalue_ref[HD:, span]
            dkv_ref[index] = jnp.concatenate([dkeys, dvalues], 0).T.astype(BF16)


def attend_back_call(place, q, do, logs, deltas, routes, h, dlogits, kv, weights, tile=128):
    slots, rows, _ = q.shape
    count = kv.shape[0] * kv.shape[1]
    width = h.shape[1]
    whole = lambda shape: pl.BlockSpec(shape, lambda i, s: (0,) * len(shape))
    by_slot = pl.BlockSpec((slots, tile, LANES), lambda i, s: (0, i, 0))
    by_row = lambda cols: pl.BlockSpec((tile, cols), lambda i, s: (i, 0))
    return pl.pallas_call(
        attend_back_kernel,
        grid_spec=pltpu.PrefetchScalarGridSpec(
            num_scalar_prefetch=1,
            grid=(rows // tile,),
            in_specs=[
                by_slot, by_slot, by_row(LANES), by_row(LANES), by_row(TOPK), by_row(width), by_row(LANES),
                whole(kv.shape), whole(weights.shape),
            ],
            out_specs=[by_row(width), whole((width, SPAN)), whole(kv.shape)],
            scratch_shapes=[
                pltpu.VMEM((count, LANES), BF16),
                pltpu.VMEM((count, LANES), BF16),
                pltpu.VMEM((slots * tile, LANES), F32),
                pltpu.VMEM((LANES, count), F32),
                pltpu.VMEM((LANES, count), F32),
                pltpu.VMEM((rows, SPAN), BF16),
                pltpu.VMEM((width, rows), BF16),
            ],
        ),
        out_shape=[
            jax.ShapeDtypeStruct((rows, width), F32),
            jax.ShapeDtypeStruct((width, SPAN), BF16),
            jax.ShapeDtypeStruct(kv.shape, BF16),
        ],
        compiler_params=pltpu.CompilerParams(vmem_limit_bytes=VMEM),
        cost_estimate=pl.CostEstimate(
            flops=10 * slots * rows * count * LANES, bytes_accessed=8 * slots * rows * LANES, transcendentals=0
        ),
        name="attend_back",
    )(place, q, do, logs, deltas, routes, h, dlogits, kv, weights)


def middle_kernel(
    x_ref, dy_ref, o_ref, gate_ref, routes_ref, tail_ref, wo_ref, w1_ref, w2_ref,
    out_ref, dmid_ref, do_ref, delta_ref, dlog_ref, g1_ref, g2_ref, go_ref, gain_ref,
    s1_ref, s2_ref, so_ref,
):
    step = pl.program_id(0)
    tile = x_ref.shape[0]
    gain = gains_of(tail_ref[...])[E + 1 : E + 2]
    routes = routes_ref[...]
    gates = gate_ref[...]
    lane = lane_index(tile)
    half = (lane >= HD).astype(jnp.int32)
    chosen = [column(routes, slot, tile) - half for slot in range(TOPK)]
    weighted = [column(gates, slot, tile) * o_ref[slot] for slot in range(TOPK)]
    parts = []
    for pair in range(PAIRS):
        total = jnp.zeros((tile, LANES), F32)
        for slot in range(TOPK):
            total = jnp.where(chosen[slot] == 2 * pair, weighted[slot], total)
        parts.append(total.astype(BF16))
    combined = jnp.concatenate(parts, 1)
    mid = x_ref[...].astype(F32) + dot_last(combined, wo_ref[...])
    normal, factor = standardize(mid)
    h2 = (normal * gain).astype(BF16)
    pre = dot(h2, w1_ref[...])
    sigma = jax.nn.sigmoid(pre)
    act = (pre * sigma).astype(BF16)
    out_ref[...] = (mid + dot_last(act, w2_ref[...])).astype(BF16)
    dy = dy_ref[...]
    dact = dot(dy, w2_ref[...])
    dpre = (dact * (sigma * (1.0 + pre * (1.0 - sigma)))).astype(BF16)
    dh2 = dot_last(dpre, w1_ref[...])
    dmid = dy.astype(F32) + norm_back(dh2 * gain, normal, factor)
    dmid_ref[...] = dmid
    dmid_b = dmid.astype(BF16)
    dcomb = dot(dmid_b, wo_ref[...])
    p1 = dot(turned(h2), dpre)
    p2 = dot(turned(dy), act)
    po = dot(turned(dmid_b), combined)
    pg = jnp.sum(dh2 * normal, 0, keepdims=True)

    @pl.when(step == 0)
    def _():
        s1_ref[...] = p1
        s2_ref[...] = p2
        so_ref[...] = po
        gain_ref[...] = pg

    @pl.when(step > 0)
    def _():
        s1_ref[...] += p1
        s2_ref[...] += p2
        so_ref[...] += po
        gain_ref[...] += pg

    weighted_total = jnp.zeros((tile, 1), F32)
    gate_grads = []
    deltas = jnp.zeros((tile, LANES), F32)
    for slot in range(TOPK):
        picked = pick_pairs(dcomb, chosen[slot])
        o = o_ref[slot]
        gate = column(gates, slot, tile)
        do = (gate * picked).astype(BF16)
        do_ref[slot] = do
        deltas = jnp.where(lane == slot, jnp.sum(o * do.astype(F32), -1, keepdims=True), deltas)
        gate_grad = jnp.sum(o * picked, -1, keepdims=True)
        gate_grads.append(gate_grad)
        weighted_total = weighted_total + gates[:, slot : slot + 1] * gate_grad
    delta_ref[...] = deltas
    dlogits = jnp.zeros((tile, LANES), F32)
    for slot in range(TOPK):
        dsel = gates[:, slot : slot + 1] * (gate_grads[slot] - weighted_total)
        dlogits = jnp.where(lane == column(routes, slot, tile), dsel, dlogits)
    dlog_ref[...] = dlogits.astype(BF16)

    @pl.when(step == pl.num_programs(0) - 1)
    def _():
        g1_ref[...] = s1_ref[...].astype(BF16)
        g2_ref[...] = s2_ref[...].astype(BF16)
        go_ref[...] = so_ref[...].astype(BF16)


def middle_call(x, dy, o, gates, routes, tail, wo, w1, w2, tile=256):
    rows, width = x.shape
    hidden = w1.shape[1]
    whole = lambda shape: pl.BlockSpec(shape, lambda i: (0,) * len(shape))
    by_slot = pl.BlockSpec((TOPK, tile, LANES), lambda i: (0, i, 0))
    by_row = lambda cols: pl.BlockSpec((tile, cols), lambda i: (i, 0))
    return pl.pallas_call(
        middle_kernel,
        grid=(rows // tile,),
        in_specs=[
            by_row(width), by_row(width), by_slot, by_row(LANES), by_row(TOPK),
            whole(tail.shape), whole(wo.shape), whole(w1.shape), whole(w2.shape),
        ],
        out_specs=[
            by_row(width), by_row(width), by_slot, by_row(LANES), by_row(LANES),
            whole((width, hidden)), whole((width, hidden)), whole((width, SPAN)), whole((1, width)),
        ],
        out_shape=[
            jax.ShapeDtypeStruct((rows, width), BF16),
            jax.ShapeDtypeStruct((rows, width), F32),
            jax.ShapeDtypeStruct((TOPK, rows, LANES), BF16),
            jax.ShapeDtypeStruct((rows, LANES), F32),
            jax.ShapeDtypeStruct((rows, LANES), BF16),
            jax.ShapeDtypeStruct((width, hidden), BF16),
            jax.ShapeDtypeStruct((width, hidden), BF16),
            jax.ShapeDtypeStruct((width, SPAN), BF16),
            jax.ShapeDtypeStruct((1, width), F32),
        ],
        scratch_shapes=[
            pltpu.VMEM((width, hidden), F32),
            pltpu.VMEM((width, hidden), F32),
            pltpu.VMEM((width, SPAN), F32),
        ],
        compiler_params=pltpu.CompilerParams(vmem_limit_bytes=VMEM),
        cost_estimate=pl.CostEstimate(
            flops=2 * rows * width * (6 * hidden + 3 * SPAN), bytes_accessed=16 * rows * width, transcendentals=0
        ),
        name="middle",
    )(x, dy, o, gates, routes, tail, wo, w1, w2)


def post_kernel(x_ref, h_ref, dmid_ref, dh_ref, dkv_ref, dlog_ref, gain2_ref, w_ref, grad_ref, gk_ref):
    gain = gains_of(w_ref[:, LANES:])[E : E + 1]
    normal, factor = standardize(x_ref[...].astype(F32))
    dkv = dkv_ref[...]
    dh = dh_ref[...] + dot_last(dkv, w_ref[:, :LANES])
    grad_ref[...] = (dmid_ref[...] + norm_back(dh * gain, normal, factor)).astype(grad_ref.dtype)
    gain1 = jnp.sum(dh * normal, 0, keepdims=True)
    width = gain1.shape[1]
    row = lax.broadcasted_iota(jnp.int32, (LANES, width), 0)
    gains = jnp.where(row == E, gain1, jnp.where(row == E + 1, gain2_ref[...], 0.0))
    h_turned = turned(h_ref[...])
    gk_ref[:, :LANES] = dot(h_turned, dkv).astype(BF16)
    gk_ref[:, LANES:] = (dot(h_turned, dlog_ref[...]) + gains.T).astype(BF16)


def post_call(x, h, dmid, dh, dkv, dlogits, gain2, weights):
    rows, width = x.shape
    return pl.pallas_call(
        post_kernel,
        out_shape=[
            jax.ShapeDtypeStruct((rows, width), BF16),
            jax.ShapeDtypeStruct((width, 2 * LANES), BF16),
        ],
        compiler_params=pltpu.CompilerParams(vmem_limit_bytes=VMEM),
        cost_estimate=pl.CostEstimate(
            flops=6 * rows * width * LANES, bytes_accessed=16 * rows * width, transcendentals=0
        ),
        name="finish",
    )(x, h, dmid, dh, dkv, dlogits, gain2, weights)


RING = ((0, 1), (1, 2), (2, 3), (3, 0))
SWAP = ((1, 3), (3, 1))


def deal(rows, place):
    half = rows.shape[0] // 2
    outer = (place == 0) | (place == 3)
    first = lax.dynamic_slice_in_dim(rows, jnp.where(outer, half, 0), half, 0)
    second = lax.dynamic_slice_in_dim(rows, jnp.where(place == 1, half, 0), half, 0)
    ring = lax.ppermute(first, "mp", RING)
    swap = lax.ppermute(second, "mp", SWAP)
    low = jnp.where(place == 0, rows[:half], jnp.where(place == 3, swap, ring))
    high = jnp.where(place == 2, rows[half:], jnp.where(place == 1, swap, ring))
    return jnp.concatenate([low, high], 0)


def gather_back(rows, place):
    half = rows.shape[0] // 2
    outer = (place == 0) | (place == 3)
    first = lax.dynamic_slice_in_dim(rows, jnp.where(outer, half, 0), half, 0)
    second = lax.dynamic_slice_in_dim(rows, jnp.where(place == 1, half, 0), half, 0)
    ring = lax.ppermute(first, "mp", tuple((b, a) for a, b in RING))
    swap = lax.ppermute(second, "mp", SWAP)
    top = jnp.where(place == 0, rows[:half], jnp.where(place == 3, swap, ring))
    bottom = jnp.where(place == 2, rows[half:], jnp.where(place == 1, swap, ring))
    return jnp.concatenate([top, bottom], 0)


def rate_columns(rates):
    return jnp.concatenate(
        [
            jnp.full((SPAN,), rates[0]),
            jnp.full((SPAN,), rates[1]),
            jnp.full((2 * HD,), rates[2]),
            jnp.full((E,), rates[3]),
            jnp.full((2,), rates[4]),
        ]
    )


def decay_columns():
    return jnp.concatenate([jnp.full((AC - 2,), WEIGHT_DECAY, F32), jnp.zeros((2,), F32)])


def adam_step(param, first, second, grad, rate, decay):
    first_new = BETA_FIRST * first + (1.0 - BETA_FIRST) * grad
    second_new = BETA_SECOND * second + (1.0 - BETA_SECOND) * grad * grad
    first_hat = first_new / (1.0 - BETA_FIRST**ADAM_STEP)
    second_hat = second_new / (1.0 - BETA_SECOND**ADAM_STEP)
    param_new = param - rate * (first_hat / (jnp.sqrt(second_hat) + ADAM_EPS) + decay * param)
    return (second_new, param_new)


ALL = ("dp", "mp")


def shards(
    tokens, cotangent, routes, starts, attn_param, attn_first, attn_second, ffn_param, ffn_first, ffn_second, rates
):
    local_rows, width = tokens.shape
    place = lax.axis_index("mp")
    devices = lax.axis_size("mp")
    groups = lax.axis_size("dp")
    block = local_rows // 2

    attn_b = attn_param.astype(BF16)
    pad = jnp.zeros((attn_b.shape[0], 2 * LANES - (AC - 2 * SPAN)), BF16)
    front = jnp.concatenate([attn_b[:, :SPAN], attn_b[:, 2 * SPAN :], pad], 1)
    front_full = lax.all_gather(front, ALL, axis=0, tiled=True)
    wo_full = lax.all_gather(attn_b[:, SPAN : 2 * SPAN], ALL, axis=0, tiled=True)
    ffn_all = lax.all_gather(ffn_param.astype(BF16), ALL, axis=0, tiled=False)
    _, depth, cols = ffn_param.shape
    ffn_all = ffn_all.reshape(groups, devices, 2, depth, cols).transpose(2, 0, 3, 1, 4)
    ffn_all = ffn_all.reshape(2, groups * depth, devices * cols)

    x = deal(tokens, place)
    dy = deal(cotangent, place)
    marks = deal(jnp.concatenate([routes, starts[:, None]], 1), place)
    routes_x = marks[:, :TOPK]
    tile = 128
    tiles = local_rows // tile
    index = jnp.arange(tiles, dtype=jnp.int32)
    low = index < tiles // 2
    here = jnp.where(low, place * block + index * tile, (2 * devices - 1 - place) * block + (index - tiles // 2) * tile)
    lower = jnp.where(low, marks[0, TOPK], marks[block, TOPK])
    where = jnp.stack([here.astype(jnp.int32), lower.astype(jnp.int32)])

    h, q, kv, gates = pre_call(x, routes_x, front_full)
    kv_all = lax.all_gather(kv, "mp", axis=0, tiled=True).reshape(2 * devices, block, LANES)
    o, logs = attend_call(where, q, kv_all, tile)
    tail = front_full[:, SPAN + LANES :]
    out, dmid, do, deltas, dlogits, g1, g2, go, gain2 = middle_call(
        x, dy, o, gates, routes_x, tail, wo_full, ffn_all[0], ffn_all[1]
    )
    layer_out = gather_back(out, place)
    dh, gq, dkv = attend_back_call(where, q, do, logs, deltas, routes_x, h, dlogits, kv_all, front_full, tile)
    dkv = lax.psum_scatter(dkv.reshape(devices * local_rows, LANES), "mp", scatter_dimension=0, tiled=True)
    grad, gk = post_call(x, h, dmid, dh, dkv, dlogits, gain2, front_full[:, SPAN:])
    input_grad = gather_back(grad, place).astype(F32)

    ffn_local = jnp.stack([g1, g2]).reshape(2, groups, depth, devices, cols).transpose(1, 3, 0, 2, 4)
    ffn_local = ffn_local.reshape(groups * devices * 2 * depth, cols)
    ffn_raw = lax.psum_scatter(ffn_local, ALL, scatter_dimension=0, tiled=True).astype(F32).reshape(2, depth, cols)
    go_raw = lax.psum_scatter(go, ALL, scatter_dimension=0, tiled=True).astype(F32)
    gq_raw = lax.psum_scatter(jnp.concatenate([gq, gk], 1), ALL, scatter_dimension=0, tiled=True).astype(F32)
    attn_raw = jnp.concatenate([gq_raw[:, :SPAN], go_raw, gq_raw[:, SPAN : SPAN + AC - 2 * SPAN]], 1)

    squares = jnp.sum(attn_raw * attn_raw) + jnp.sum(ffn_raw * ffn_raw)
    grad_norm = jnp.sqrt(lax.psum(squares, ALL))
    factor = jnp.minimum(1.0, CLIP_NORM / grad_norm)
    attn_grad = attn_raw * factor
    ffn_grad = ffn_raw * factor
    attn_second_new, attn_new = adam_step(
        attn_param, attn_first, attn_second, attn_grad, rate_columns(rates)[None, :], decay_columns()[None, :]
    )
    ffn_rates = jnp.stack([rates[5], rates[6]])[:, None, None]
    ffn_second_new, ffn_new = adam_step(ffn_param, ffn_first, ffn_second, ffn_grad, ffn_rates, WEIGHT_DECAY)
    return (
        layer_out,
        input_grad,
        attn_grad,
        attn_second_new,
        attn_new,
        ffn_grad,
        ffn_second_new,
        ffn_new,
        grad_norm,
        attn_grad[:, AC - 2 :],
    )


def solution(mesh):
    by_row = P(ALL, None)
    by_ffn = P(None, "dp", "mp")
    return jax.shard_map(
        shards,
        mesh=mesh,
        in_specs=(by_row, by_row, by_row, P(ALL), by_row, by_row, by_row, by_ffn, by_ffn, by_ffn, P()),
        out_specs=(by_row, by_row, by_row, by_row, by_row, by_ffn, by_ffn, by_ffn, P(), by_row),
        check_vma=False,
    )
```

time: 1710 us -> 790 us (0.46)
  matrix products: 531 us -> 0 us
  local copies, waits for them, and re-layouts: 534 us -> 41.7 us
  other arithmetic: 223 us -> 21.2 us
  waiting for transfers between devices: 317 us -> 483 us
  Pallas kernels: 0 us -> 163 us
  loops' own time: 22.8 us -> 0 us
    dot_general x132 -> x0, matrix products: 531 us -> none  [the longest x54 231 us: contract_last(): lax.dot_general(left, right, (((1,), (1,)), ((), ())), preferred_element_...]
    gather x10 -> x0, local copies, waits for them, and re-layouts: 290 us -> none  [the longest x2 124 us: shards(): picked = jnp.take_along_axis(combined_grad, routes[:, :, None], axis=1)]
    reduce_scatter x4, waiting for transfers between devices: 171 us -> 350 us  [the longest x1 137 us: shards(): lax.psum_scatter(ffn_local, ALL, scatter_dimension=0, tiled=True)]
    convert_element_type x22 -> x4, other arithmetic: 169 us -> 4.12 us  [the longest x1 1.61 us: shards(): input_grad = gather_back(grad, place).astype(F32)]
    pallas_call x0 -> x5, Pallas kernels: none -> 163 us  [the longest x1 62.4 us: attend_back_call(): pl.pallas_call(attend_back_kernel, grid_spec=pltpu.PrefetchScalarGridSpec...]
    dynamic_slice x112 -> x4, local copies, waits for them, and re-layouts: 69.9 us -> 5.49 us  [the longest x2 3.39 us: deal(): first = lax.dynamic_slice_in_dim(rows, jnp.where(outer, half, 0), half, 0)]
    dynamic_update_slice x48 -> x0, local copies, waits for them, and re-layouts: 62.8 us -> none  [shards(): attended, log_total = lax.map(forward_block, jnp.arange(blocks))]
    reduce_sum x24 -> x0, other arithmetic: 31.8 us -> none  [the longest x16 20.5 us: forward_block(): total = jnp.sum(expo, -1)]
  transfers between devices with their start and end apart: 10 -> 18, of which waited for: 7 -> 12; matrix products, arithmetic and copies ran while one was open for 33% -> 7% of each run, Pallas kernels for 0% -> 6%
where the time goes in v1:
time: 790 us; the launch traced here: 784 us
  waiting for transfers between devices  483 us (61%)
  Pallas kernels  163 us (21%)
  local copies, waits for them, and re-layouts  41.7 us (5%)
  blocking collectives  41.6 us (5%)
  other arithmetic  21.2 us (3%)
  between operations  18.3 us (2%)
  starting transfers between devices  15.2 us (2%)
    reduce_scatter x1, waiting for transfers between devices, shards(): lax.psum_scatter(ffn_local, ALL, scatter_dimension=0, tiled=True)  137 us
    reduce_scatter x1, waiting for transfers between devices, shards(): lax.psum_scatter(jnp.concatenate([gq, gk], 1), ALL, scatter_dimension=0,...  133 us
    pallas_call x1, Pallas kernels, attend_back_call(): pl.pallas_call(attend_back_kernel, grid_spec=pltpu.PrefetchScalarGridSpec...  62.4 us
    reduce_scatter x1, waiting for transfers between devices, shards(): lax.psum_scatter(go, ALL, scatter_dimension=0, tiled=True).astype(F32)  59.1 us
    pallas_call x1, Pallas kernels, middle_call(): pl.pallas_call(middle_kernel, grid=(rows // tile,), in_specs=[by_row(widt...  46.6 us
    all_gather x1, waiting for transfers between devices, shards(): wo_full = lax.all_gather(attn_b[:, SPAN:2 * SPAN], ALL, axis=0, tiled=True)  45.7 us
    psum x1, blocking collectives, shards(): grad_norm = jnp.sqrt(lax.psum(squares, ALL))  41.6 us
    pallas_call x1, Pallas kernels, attend_call(): pl.pallas_call(attend_kernel, grid_spec=pltpu.PrefetchScalarGridSpec(num_...  37.3 us
  transfers between devices with their start and end apart: 18, of which 12 were waited for; matrix products, arithmetic and copies ran while one was open for 7% of the time, Pallas kernels for 6%

profile of v1, /device:TPU:1, one launch (start us, length us, event | category | flops | bytes accessed | tf_op | source)
XLA Modules:
  0.0 783.6 jit_solution(12088708806171629200)
XLA Ops:
  9.7 2.3 constant_dynamic-slice_fusion.6
  12.1 3.9 collective-permute-start
  19.2 3.4 collective-permute-start.4
  22.5 19.0 %collective-permute-done.4 = s32[512,9]{0,1:T(8,128)S(1)} collective-permute-done((s32[512,9]{0,1:T(8,128)S(1)}, s32[512,9]{0,1:T(8,128)S(1)}, u32[]{:S(2)}, u32[]{:S(2)}) %collective-permute-start.4) | collective-permute-done | bytes 18464 | tf_op jit(solution)/shard_map/ppermute | solution.py:550
  47.5 22.8 %all-gather.6.cloned.1.call-done.w_ref = bf16[512,1792]{1,0:T(8,128)(2,1)} async-done(((bf16[16,1792]{1,0:T(8,128)(2,1)}), bf16[512,1792]{1,0:T(8,128)(2,1)}) %all-gather.6.cloned.1.call-update) | async-done | bytes 1835024 | tf_op jit(solution)/shard_map/all_gather | solution.py:608
  70.3 10.2 %project.1 = (bf16[1024,512]{1,0:T(8,128)(2,1)}, bf16[8,1024,128]{2,1,0:T(8,128)(2,1)}, bf16[1024,128]{1,0:T(8,128)(2,1)}, f32[1024,128]{1,0:T(8,128)}) custom-call(bf16[1024,512]{1,0:T(8,128)(2,1)} %pad_maximum_fusion.2.x_ref, s32[1024,8]{1,0:T(8,128)} %copy.35.routes_ref, bf16[512,1792]{1,0:T(8,128)(2,1)} %all-gather.6.cloned.1.call-done.w_ref), custom_call_target="tpu_custom_call" | custom-call | flops 1879048192 | bytes 6029312 | tf_op jit(solution)/shard_map/project/pallas_call | solution.py:113
  87.6 8.6 %all-gather.8.cloned.1.call-done = bf16[4096,128]{1,0:T(8,128)(2,1)} async-done(((bf16[1024,128]{1,0:T(8,128)(2,1)}), bf16[4096,128]{1,0:T(8,128)(2,1)}) %all-gather.8.cloned.1.call-update) | async-done | bytes 1048592 | tf_op jit(solution)/shard_map/all_gather | solution.py:628
  96.3 37.3 %attend.1 = (f32[8,1024,128]{2,1,0:T(8,128)}, f32[1024,128]{1,0:T(8,128)}) custom-call(s32[2,8]{1,0:T(2,128)} %pad_add_fusion.2.place_ref, bf16[8,1024,128]{2,1,0:T(8,128)(2,1)} %get-tuple-element.30.q_ref, bf16[8,512,128]{2,1,0:T(8,128)(2,1)} %bitcast.36), custom_call_target="tpu_custom_call" | custom-call | flops 34359738368 | bytes 8388608 | tf_op jit(solution)/shard_map/attend/pallas_call | solution.py:231
  133.6 28.4 %all-gather.12.cloned.1.call-done = bf16[64,64,512]{2,1,0:T(8,128)(2,1)} async-done(((bf16[2,64,512]{2,1,0:T(8,128)(2,1)}), bf16[64,64,512]{2,1,0:T(8,128)(2,1)}) %all-gather.12.cloned.1.call-update) | async-done | bytes 4194320 | tf_op jit(solution)/shard_map/all_gather | solution.py:610
  162.0 5.7 copy.39
  173.1 45.7 %all-gather.10.cloned.1.call-done.wo_ref = bf16[512,1536]{1,0:T(8,128)(2,1)} async-done(((bf16[16,1536]{1,0:T(8,128)(2,1)}), bf16[512,1536]{1,0:T(8,128)(2,1)}) %all-gather.10.cloned.1.call-update) | async-done | bytes 1572880 | tf_op jit(solution)/shard_map/all_gather | solution.py:609
  218.8 46.6 %middle.1 = (bf16[1024,512]{1,0:T(8,128)(2,1)}, f32[1024,512]{1,0:T(8,128)}, bf16[8,1024,128]{2,1,0:T(8,128)(2,1)}, f32[1024,128]{1,0:T(8,128)}, bf16[1024,128]{...) custom-call(bf16[1024,512]{1,0:T(8,128)(2,1)} %pad_maximum_fusion.2., ...), custom_call_target="tpu_custom_call" | custom-call | flops 17716740096 | bytes 8388608 | tf_op jit(solution)/shard_map/middle/pallas_call | solution.py:474
  265.4 62.4 %attend_back.1 = (f32[1024,512]{1,0:T(8,128)}, bf16[512,1536]{1,0:T(8,128)(2,1)}, bf16[8,512,128]{2,1,0:T(8,128)(2,1)}) custom-call(s32[2,8]{1,0:T(2,128)} %pad_add_fusion.2.place_ref, bf16[8,1024,128]{2,1,0:T(8,128)(2,1)} %get-tuple-element.30.q_ref, bf16[8,1024,128]{2,1,0:T(8,128)(2,1)} %get-tuple-element.37.do_ref, ...), custom_call_target="tpu_custom_call" | custom-call | flops 42949672960 | bytes 8388608 | tf_op jit(solution)/shard_map/attend_back/pallas_call | solution.py:353
  330.2 21.2 %reduce-scatter.5.cloned.1.call-done.dkv_ref = bf16[1024,128]{1,0:T(8,128)(2,1)} async-done(((bf16[4096,128]{1,0:T(8,128)(2,1)}), bf16[1024,128]{1,0:T(8,128)(2,1)}) %reduce-scatter.5.cloned.1.call-update) | async-done | bytes 262160 | tf_op jit(solution)/shard_map/reduce_scatter | solution.py:636
  351.4 6.2 finish.1
  359.9 3.3 stack.18
  365.1 3.3 stack.19
  370.1 2.3 pad_maximum_fusion
  378.0 3.2 collective-permute-start.8
  385.2 4.5 collective-permute-done.6
  393.7 59.1 %reduce-scatter.9.cloned.1.call-done = bf16[16,1536]{1,0:T(8,128)(2,1)} async-done(((bf16[512,1536]{1,0:T(8,128)(2,1)}), bf16[16,1536]{1,0:T(8,128)(2,1)}) %reduce-scatter.9.cloned.1.call-update) | async-done | bytes 49168 | tf_op jit(solution)/shard_map/reduce_scatter | solution.py:643
  453.8 132.9 %reduce-scatter.7.cloned.1.call-done = bf16[16,1792]{1,0:T(8,128)(2,1)} async-done(((bf16[512,1792]{1,0:T(8,128)(2,1)}), bf16[16,1792]{1,0:T(8,128)(2,1)}) %reduce-scatter.7.cloned.1.call-update) | async-done | bytes 57360 | tf_op jit(solution)/shard_map/reduce_scatter | solution.py:644
  588.8 136.8 %reduce-scatter.11.cloned.1.call-done = bf16[128,512]{1,0:T(8,128)(2,1)} async-done(((bf16[4096,512]{1,0:T(8,128)(2,1)}), bf16[128,512]{1,0:T(8,128)(2,1)}) %reduce-scatter.11.cloned.1.call-update) | async-done | bytes 131088 | tf_op jit(solution)/shard_map/reduce_scatter | solution.py:642
  730.1 41.6 %psum.7 = f32[]{:T(128)} all-reduce(f32[]{:T(128)S(6)} %add.91), channel_id=1, replica_groups=mesh['dp'=8,'mp'=4] {'dp','mp'}, use_global_device_ids=true, to_apply=%region_6.7 | all-reduce | flops 1 | bytes 8 | tf_op jit(solution)/shard_map/psum | solution.py:648
  (124 shorter events, 54.6 us)
Async XLA Ops:
  7.2 63.1 %all-gather.6.cloned.1.call-start = ((), (), s32[]{:S(2)}) async-start(), calls=%async_computation.4 | async-start | bytes 1892352 | tf_op jit(solution)/shard_map/all_gather | solution.py:608
  9.6 86.6 %all-gather.8.cloned.1.call-start = ((), (), s32[]{:S(2)}) async-start(), calls=%async_computation.5 | async-start | bytes 1310720 | tf_op jit(solution)/shard_map/all_gather | solution.py:628
  12.1 31.7 %collective-permute-start = (bf16[512,512]{1,0:T(8,128)(2,1)}, bf16[512,512]{1,0:T(8,128)(2,1)S(1)}, u32[]{:S(2)}, u32[]{:S(2)}) collective-permute-start(bf16[512,512]{1,0:T(8,128)(2,1)} %get-tuple-element.102), channel_id=1, source_target_pairs={{1,3},{3,1},{5,7},{7,5},{9,11},{11,9},{13,15},{15,13},{17,19},{19,... | collective-permute-start | bytes 1572872 | tf_op jit(solution)/shard_map/ppermute | solution.py:550
  16.0 27.7 %collective-permute-start.1 = (bf16[512,512]{1,0:T(8,128)(2,1)}, bf16[512,512]{1,0:T(8,128)(2,1)S(1)}, u32[]{:S(2)}, u32[]{:S(2)}) collective-permute-start(bf16[512,512]{1,0:T(8,128)(2,1)} %get-tuple-element.101), channel_id=1, source_target_pairs={{0,1},{1,2},{2,3},{3,0},{4,5},{5,6},{6,7},{7,4},{8,9},{9,10},{10,1... | collective-permute-start | bytes 1572872 | tf_op jit(solution)/shard_map/ppermute | solution.py:549
  17.1 26.6 %collective-permute-start.2 = (bf16[512,512]{1,0:T(8,128)(2,1)}, bf16[512,512]{1,0:T(8,128)(2,1)}, u32[]{:S(2)}, u32[]{:S(2)}) collective-permute-start(bf16[512,512]{1,0:T(8,128)(2,1)} %get-tuple-element.100), channel_id=1, source_target_pairs={{1,3},{3,1},{5,7},{7,5},{9,11},{11,9},{13,15},{15,13},{17,19},{19,... | collective-permute-start | bytes 1572872 | tf_op jit(solution)/shard_map/ppermute | solution.py:550
  19.1 25.7 %collective-permute-start.3 = (bf16[512,512]{1,0:T(8,128)(2,1)}, bf16[512,512]{1,0:T(8,128)(2,1)}, u32[]{:S(2)}, u32[]{:S(2)}) collective-permute-start(bf16[512,512]{1,0:T(8,128)(2,1)} %get-tuple-element.99), channel_id=1, source_target_pairs={{0,1},{1,2},{2,3},{3,0},{4,5},{5,6},{6,7},{7,4},{8,9},{9,10},{10,1... | collective-permute-start | bytes 1572872 | tf_op jit(solution)/shard_map/ppermute | solution.py:549
  19.2 22.4 %collective-permute-start.4 = (s32[512,9]{0,1:T(8,128)S(1)}, s32[512,9]{0,1:T(8,128)S(1)}, u32[]{:S(2)}, u32[]{:S(2)}) collective-permute-start(s32[512,9]{0,1:T(8,128)S(1)} %get-tuple-element.108), channel_id=1, source_target_pairs={{1,3},{3,1},{5,7},{7,5},{9,11},{11,9},{13,15},{15,13},{17,19},{19,... | collective-permute-start | bytes 55304 | tf_op jit(solution)/shard_map/ppermute | solution.py:550
  41.5 1.2 collective-permute-start.5
  80.5 81.5 %all-gather.12.cloned.1.call-start = ((), (), s32[]{:S(2)}) async-start(), calls=%async_computation.11 | async-start | bytes 4325376 | tf_op jit(solution)/shard_map/all_gather | solution.py:610
  81.3 137.5 %all-gather.10.cloned.1.call-start = ((), (), s32[]{:S(2)}) async-start(), calls=%async_computation.6 | async-start | bytes 1622016 | tf_op jit(solution)/shard_map/all_gather | solution.py:609
  81.9 269.5 %reduce-scatter.5.cloned.1.call-start = ((), (), s32[]{:S(2)}) async-start(), calls=%async_computation.7 | async-start | bytes 1310720 | tf_op jit(solution)/shard_map/reduce_scatter | solution.py:636
  327.9 124.9 %reduce-scatter.9.cloned.1.call-start = ((), (), s32[]{:S(2)}) async-start(), calls=%async_computation.9 | async-start | bytes 1622016 | tf_op jit(solution)/shard_map/reduce_scatter | solution.py:643
  328.5 258.2 %reduce-scatter.7.cloned.1.call-start = ((), (), s32[]{:S(2)}) async-start(), calls=%async_computation.8 | async-start | bytes 1892352 | tf_op jit(solution)/shard_map/reduce_scatter | solution.py:644
  359.9 365.7 %reduce-scatter.11.cloned.1.call-start = ((), (), s32[]{:S(2)}) async-start(), calls=%async_computation.10 | async-start | bytes 4325376 | tf_op jit(solution)/shard_map/reduce_scatter | solution.py:642
  374.7 15.0 %collective-permute-start.6 = (bf16[512,512]{1,0:T(8,128)(2,1)}, bf16[512,512]{1,0:T(8,128)(2,1)}, u32[]{:S(2)}, u32[]{:S(2)}) collective-permute-start(bf16[512,512]{1,0:T(8,128)(2,1)} %get-tuple-element.98), channel_id=1, source_target_pairs={{1,3},{3,1},{5,7},{7,5},{9,11},{11,9},{13,15},{15,13},{17,19},{19,... | collective-permute-start | bytes 1572872 | tf_op jit(solution)/shard_map/ppermute | solution.py:562
  376.8 14.6 %collective-permute-start.7 = (bf16[512,512]{1,0:T(8,128)(2,1)}, bf16[512,512]{1,0:T(8,128)(2,1)}, u32[]{:S(2)}, u32[]{:S(2)}) collective-permute-start(bf16[512,512]{1,0:T(8,128)(2,1)} %get-tuple-element.97), channel_id=1, source_target_pairs={{1,0},{2,1},{3,2},{0,3},{5,4},{6,5},{7,6},{4,7},{9,8},{10,9},{11,1... | collective-permute-start | bytes 1572872 | tf_op jit(solution)/shard_map/ppermute | solution.py:561
  378.0 75.6 %collective-permute-start.8 = (bf16[512,512]{1,0:T(8,128)(2,1)}, bf16[512,512]{1,0:T(8,128)(2,1)S(1)}, u32[]{:S(2)}, u32[]{:S(2)}) collective-permute-start(bf16[512,512]{1,0:T(8,128)(2,1)} %get-tuple-element.96), channel_id=1, source_target_pairs={{1,3},{3,1},{5,7},{7,5},{9,11},{11,9},{13,15},{15,13},{17,19},{19,... | collective-permute-start | bytes 1572872 | tf_op jit(solution)/shard_map/ppermute | solution.py:562
  381.2 72.5 %collective-permute-start.9 = (bf16[512,512]{1,0:T(8,128)(2,1)}, bf16[512,512]{1,0:T(8,128)(2,1)S(1)}, u32[]{:S(2)}, u32[]{:S(2)}) collective-permute-start(bf16[512,512]{1,0:T(8,128)(2,1)} %get-tuple-element.95), channel_id=1, source_target_pairs={{1,0},{2,1},{3,2},{0,3},{5,4},{6,5},{7,6},{4,7},{9,8},{10,9},{11,1... | collective-permute-start | bytes 1572872 | tf_op jit(solution)/shard_map/ppermute | solution.py:561
  453.8 318.7 %copy-start.8 = (f32[16,3226]{1,0:T(8,128)S(1)}, f32[16,3226]{1,0:T(8,128)}, u32[]{:S(2)}) copy-start(f32[16,3226]{1,0:T(8,128)} %param.15) | copy-start | bytes 619396
  453.8 318.7 %copy-start.15 = (f32[16,3226]{1,0:T(8,128)S(1)}, f32[16,3226]{1,0:T(8,128)}, u32[]{:S(2)}) copy-start(f32[16,3226]{1,0:T(8,128)} %param.16) | copy-start | bytes 619396
  453.8 318.7 %copy-start.16 = (f32[16,3226]{1,0:T(8,128)S(1)}, f32[16,3226]{1,0:T(8,128)}, u32[]{:S(2)}) copy-start(f32[16,3226]{1,0:T(8,128)} %param.17) | copy-start | bytes 619396
  453.8 318.7 %copy-start.18 = (f32[3226]{0:T(1024)S(1)}, f32[3226]{0:T(1024)}, u32[]{:S(2)}) copy-start(f32[3226]{0:T(1024)} %constant.20.clone.1) | copy-start | bytes 38716
  728.5 45.7 %copy-start.12 = (f32[2,64,512]{2,1,0:T(8,128)S(1)}, f32[2,64,512]{2,1,0:T(8,128)}, u32[]{:S(2)}) copy-start(f32[2,64,512]{2,1,0:T(8,128)} %param.19) | copy-start | bytes 786436
  728.5 45.7 %copy-start.13 = (f32[2,64,512]{2,1,0:T(8,128)S(1)}, f32[2,64,512]{2,1,0:T(8,128)}, u32[]{:S(2)}) copy-start(f32[2,64,512]{2,1,0:T(8,128)} %param.20) | copy-start | bytes 786436
  (15 other events, 164.1 us)
Sparse Core Ops, SparseCore 0:
  11.4 58.8 all-gather.5
  80.6 15.5 all-gather.7
  99.7 62.2 all-gather.11
  165.3 53.4 all-gather.9
  328.0 23.3 reduce-scatter.4
  357.3 95.4 reduce-scatter.8
  455.2 131.4 reduce-scatter.6
  589.0 136.5 reduce-scatter.10
